TPU v7x, 32 devices: a whole 2x2x4 slice. The times are simulated.
32 devices in a mesh: dp: 8 (over z, x), seq: 4 (over y, core).
Axes of the slice: x: 2, y: 2, z: 4, core: 2. Of those that a mesh axis runs over, the one named last changes fastest.
Arguments:
- queries: bfloat16 [8, 512, 1024], P('dp', 'seq'), may hold values from -6 to 6
- key_vecs: bfloat16 [8, 512, 1024], P('dp', 'seq'), may hold values from -6 to 6
- value_vecs: bfloat16 [8, 512, 1024], P('dp', 'seq'), may hold values from -6 to 6
- residual_in: bfloat16 [8, 512, 1024], P('dp', 'seq'), may hold values from -8 to 8
- point_weight: bfloat16 [1024, 2048], P('seq'), may hold values from -0.5 to 0.5
- context_grad: bfloat16 [8, 512, 1024], P('dp', 'seq'), may hold values from -6 to 6
- depth_kernel: float32 [31, 1024], replicated, may hold values from -1 to 1
- norm_gain: float32 [1024], replicated, may hold values from 0.5 to 1.5
- norm_bias: float32 [1024], replicated, may hold values from -3 to 3
- conv_grad: bfloat16 [8, 512, 1024], P('dp', 'seq'), may hold values from -1.5 to 1.5
Outputs:
- context: bfloat16 [8, 512, 1024], P('dp', 'seq')
- conv_output: bfloat16 [8, 512, 1024], P('dp', 'seq')
- query_grad: bfloat16 [8, 512, 1024], P('dp', 'seq')
- key_grad: bfloat16 [8, 512, 1024], P('dp', 'seq')
- value_grad: bfloat16 [8, 512, 1024], P('dp', 'seq')
- input_grad: bfloat16 [8, 512, 2048], P('dp', 'seq')
- residual_grad: bfloat16 [8, 512, 1024], P('dp', 'seq')
- kernel_grad: float32 [31, 1024], replicated
- gain_grad: float32 [1024], replicated
- bias_grad: float32 [1024], replicated
All inputs are finite; a program needn't handle non-finite values.
Results may differ from a plain program's by a relative error of at most 0.0049.
The roundings to bfloat16 on the way count: a program that leaves them out, or rounds other values in their place, can miss the bound.
Values may be sent and summed in bfloat16 or wider, within the bound.
A program may use at most 64 MiB of HBM per device.

v0:
```python
import jax
import jax.numpy as jnp
from jax import lax
from jax.sharding import PartitionSpec as P

HEADS = 16


def from_behind(block, axis, distance):
    devices = range(lax.axis_size(axis))
    route = [(i - distance, i) for i in devices if i - distance in devices]
    return lax.ppermute(block, axis, route)


def block_probs(query_block, key_heads, scaling):
    scores = (
        jnp.einsum("qhd,khd->hqk", query_block, key_heads, preferred_element_type=jnp.float32)
        * scaling
    )
    shifted = jnp.exp(scores - jnp.max(scores, axis=2, keepdims=True))
    return shifted / jnp.sum(shifted, axis=2, keepdims=True)


def attend_forward(query_part, key_part, value_part, head_count):
    frames, channels = query_part.shape
    head_depth = channels // head_count
    scaling = head_depth ** (-0.5)
    query_heads = query_part.reshape(frames, head_count, head_depth)
    key_heads = key_part.reshape(frames, head_count, head_depth)
    value_heads = value_part.reshape(frames, head_count, head_depth)
    block_rows = min(512, frames)

    def one_block(running, index):
        query_block = lax.dynamic_slice_in_dim(query_heads, index * block_rows, block_rows, 0)
        rounded = block_probs(query_block, key_heads, scaling).astype(jnp.bfloat16)
        context = jnp.einsum(
            "hqk,khd->qhd", rounded, value_heads, preferred_element_type=jnp.float32
        ).astype(jnp.bfloat16)
        return (running, context)

    unused, blocks = lax.scan(
        one_block, jnp.zeros((), jnp.float32), jnp.arange(frames // block_rows)
    )
    return blocks.reshape(frames, channels)


def attend_backward(query_part, key_part, value_part, grad_part, context_part, head_count):
    frames, channels = query_part.shape
    head_depth = channels // head_count
    scaling = head_depth ** (-0.5)
    query_heads = query_part.reshape(frames, head_count, head_depth)
    key_heads = key_part.reshape(frames, head_count, head_depth)
    value_heads = value_part.reshape(frames, head_count, head_depth)
    grad_heads = grad_part.reshape(frames, head_count, head_depth)
    context_heads = context_part.reshape(frames, head_count, head_depth)
    block_rows = min(512, frames)

    def one_block(running, index):
        key_total, value_total = running
        start = index * block_rows
        query_block = lax.dynamic_slice_in_dim(query_heads, start, block_rows, 0)
        grad_block = lax.dynamic_slice_in_dim(grad_heads, start, block_rows, 0)
        context_block = lax.dynamic_slice_in_dim(context_heads, start, block_rows, 0)
        probabilities = block_probs(query_block, key_heads, scaling)
        rounded = probabilities.astype(jnp.bfloat16)
        row_dots = jnp.sum(
            grad_block.astype(jnp.float32) * context_block.astype(jnp.float32), axis=2
        )
        prob_grad = jnp.einsum(
            "qhd,khd->hqk", grad_block, value_heads, preferred_element_type=jnp.float32
        )
        score_grad = (probabilities * (prob_grad - row_dots.T[:, :, None]) * scaling).astype(
            jnp.bfloat16
        )
        query_grad = jnp.einsum(
            "hqk,khd->qhd", score_grad, key_heads, preferred_element_type=jnp.float32
        ).astype(jnp.bfloat16)
        key_total = key_total + jnp.einsum(
            "hqk,qhd->khd", score_grad, query_block, preferred_element_type=jnp.float32
        )
        value_total = value_total + jnp.einsum(
            "hqk,qhd->khd", rounded, grad_block, preferred_element_type=jnp.float32
        )
        return ((key_total, value_total), query_grad)

    empty = jnp.zeros((frames, head_count, head_depth), jnp.float32)
    totals, blocks = lax.scan(one_block, (empty, empty), jnp.arange(frames // block_rows))
    query_grad = blocks.reshape(frames, channels)
    key_grad = totals[0].astype(jnp.bfloat16).reshape(frames, channels)
    value_grad = totals[1].astype(jnp.bfloat16).reshape(frames, channels)
    return (query_grad, key_grad, value_grad)


def shards(
    queries,
    key_vecs,
    value_vecs,
    residual_in,
    point_weight,
    context_grad,
    depth_kernel,
    norm_gain,
    norm_bias,
    conv_grad,
):
    head_count = HEADS // lax.axis_size("seq")
    query_heads, key_heads, value_heads = (
        lax.all_to_all(queries, "seq", split_axis=2, concat_axis=1, tiled=True),
        lax.all_to_all(key_vecs, "seq", split_axis=2, concat_axis=1, tiled=True),
        lax.all_to_all(value_vecs, "seq", split_axis=2, concat_axis=1, tiled=True),
    )
    context_local = attend_forward(query_heads[0], key_heads[0], value_heads[0], head_count)
    context_out = lax.all_to_all(
        context_local[None], "seq", split_axis=1, concat_axis=2, tiled=True
    )
    taps = depth_kernel.shape[0]
    channels = depth_kernel.shape[1]
    span = taps - 1
    frames = residual_in.shape[1]
    mixed = (residual_in[0].astype(jnp.float32) + context_out[0].astype(jnp.float32)).astype(
        jnp.bfloat16
    )
    pre_conv = jnp.dot(
        mixed,
        lax.all_gather(point_weight, "seq", axis=0, tiled=True),
        preferred_element_type=jnp.float32,
    )
    conv_input = pre_conv.astype(jnp.bfloat16)[None]
    value_half = conv_input[:, :, :channels].astype(jnp.float32)
    gate_sig = jax.nn.sigmoid(conv_input[:, :, channels:].astype(jnp.float32))
    glu = (value_half * gate_sig).astype(jnp.bfloat16)
    earlier = from_behind(glu[:, frames - span :], "seq", 1)
    glu_wide = jnp.concatenate([earlier, glu], axis=1)
    glu_view = lax.optimization_barrier(glu_wide).astype(jnp.float32)
    depthwise = jnp.zeros((1, frames, channels), jnp.float32)
    for offset in range(taps):
        depthwise = depthwise + depth_kernel[offset] * glu_view[:, offset : offset + frames]
    average = jnp.mean(depthwise, axis=2, keepdims=True)
    centered = depthwise - average
    variance = jnp.mean(centered * centered, axis=2, keepdims=True)
    inverse = lax.rsqrt(variance + 1e-05)
    normed = centered * inverse
    affine = normed * norm_gain + norm_bias
    sig_affine = jax.nn.sigmoid(affine)
    conv_output = (affine * sig_affine).astype(jnp.bfloat16)
    affine_grad = conv_grad.astype(jnp.float32) * (sig_affine * (1.0 + affine * (1.0 - sig_affine)))
    gain_term = jnp.sum(affine_grad * normed, axis=(0, 1))
    bias_term = jnp.sum(affine_grad, axis=(0, 1))
    normed_grad = affine_grad * norm_gain
    depth_grad = inverse * (
        normed_grad
        - jnp.mean(normed_grad, axis=2, keepdims=True)
        - normed * jnp.mean(normed_grad * normed, axis=2, keepdims=True)
    )
    kernel_term = jnp.stack(
        [
            jnp.sum(depth_grad * glu_view[:, offset : offset + frames], axis=(0, 1))
            for offset in range(taps)
        ]
    )
    kernel_total, gain_total, bias_total = lax.psum(
        (kernel_term, gain_term, bias_term), ("dp", "seq")
    )
    recordings = lax.axis_size("dp")
    kernel_grad = kernel_total / recordings
    gain_grad = gain_total / recordings
    bias_grad = bias_total / recordings
    later = from_behind(depth_grad[:, :span], "seq", -1)
    grad_wide = jnp.concatenate([depth_grad, later], axis=1)
    glu_grad = jnp.zeros((1, frames, channels), jnp.float32)
    for offset in range(taps):
        begin = span - offset
        glu_grad = glu_grad + depth_kernel[offset] * grad_wide[:, begin : begin + frames]
    input_grad = jnp.concatenate(
        [glu_grad * gate_sig, glu_grad * value_half * gate_sig * (1.0 - gate_sig)], axis=2
    ).astype(jnp.bfloat16)
    slope_rows = input_grad[0]
    mixed_grad = jnp.einsum(
        "fc,dc->fd",
        slope_rows,
        lax.all_gather(point_weight, "seq", axis=0, tiled=True),
        preferred_element_type=jnp.float32,
    )
    residual_grad = (context_grad.astype(jnp.float32) + mixed_grad[None]).astype(jnp.bfloat16)
    grad_heads = lax.all_to_all(residual_grad, "seq", split_axis=2, concat_axis=1, tiled=True)
    query_grad, key_grad, value_grad = attend_backward(
        query_heads[0], key_heads[0], value_heads[0], grad_heads[0], context_local, head_count
    )
    query_out, key_out, value_out = (
        lax.all_to_all(query_grad[None], "seq", split_axis=1, concat_axis=2, tiled=True),
        lax.all_to_all(key_grad[None], "seq", split_axis=1, concat_axis=2, tiled=True),
        lax.all_to_all(value_grad[None], "seq", split_axis=1, concat_axis=2, tiled=True),
    )
    return (
        context_out,
        conv_output,
        query_out,
        key_out,
        value_out,
        input_grad,
        residual_grad,
        kernel_grad,
        gain_grad,
        bias_grad,
    )


def solution(mesh):
    in_specs = (
        P("dp", "seq", None),
        P("dp", "seq", None),
        P("dp", "seq", None),
        P("dp", "seq", None),
        P("seq", None),
        P("dp", "seq", None),
        P(),
        P(),
        P(),
        P("dp", "seq", None),
    )
    out_specs = (
        P("dp", "seq", None),
        P("dp", "seq", None),
        P("dp", "seq", None),
        P("dp", "seq", None),
        P("dp", "seq", None),
        P("dp", "seq", None),
        P("dp", "seq", None),
        P(),
        P(),
        P(),
    )
    return jax.shard_map(shards, mesh=mesh, in_specs=in_specs, out_specs=out_specs, check_vma=False)
```

profile of v0, /device:TPU:0, one launch (start us, length us, event | category | flops | bytes accessed | tf_op | source)
XLA Modules:
  0.0 264.9 jit_solution(9525014765251899373)
XLA Ops:
  7.9 1.3 copy.72
  9.8 2.3 reduce.5
  12.1 0.8 reshape.213
  12.9 4.2 %all-to-all-start = ((bf16[4,2,16384]{2,1,0:T(2,128)(2,1)}), bf16[4,2,16384]{2,1,0:T(2,128)(2,1)S(1)}, u32[]{:S(2)}, u32[]{:S(2)}) async-start(bf16[4,2,16384]{2,1,0:T(2,128)(2,1)} %reshape.213), calls=%async_computation | async-start | bytes 524288 | tf_op jit(solution)/shard_map/all_to_all | solution.py:108
  17.1 1.3 copy.74
  18.4 2.3 reduce.6
  20.6 0.8 reshape.215
  21.4 2.4 all-to-all-done
  23.9 3.4 %all-to-all-start.1 = ((bf16[4,2,16384]{2,1,0:T(2,128)(2,1)}), bf16[4,2,16384]{2,1,0:T(2,128)(2,1)S(1)}, u32[]{:S(2)}, u32[]{:S(2)}) async-start(bf16[4,2,16384]{2,1,0:T(2,128)(2,1)} %reshape.215), calls=%async_computation.1 | async-start | bytes 524288 | tf_op jit(solution)/shard_map/all_to_all | solution.py:109
  27.7 2.3 reduce.4
  29.9 0.8 reshape.211
  30.7 5.7 %all-to-all-done.1 = bf16[4,2,16384]{2,1,0:T(2,128)(2,1)S(1)} async-done(((bf16[4,2,16384]{2,1,0:T(2,128)(2,1)}), bf16[4,2,16384]{2,1,0:T(2,128)(2,1)S(1)}, u32[]{:S(2)}, u32[]{:S(2)}) %all-to-all-start.1) | async-done | bytes 262176 | tf_op jit(solution)/shard_map/all_to_all | solution.py:109
  36.4 3.4 %all-to-all-start.2 = ((bf16[4,2,16384]{2,1,0:T(2,128)(2,1)}), bf16[4,2,16384]{2,1,0:T(2,128)(2,1)S(1)}, u32[]{:S(2)}, u32[]{:S(2)}) async-start(bf16[4,2,16384]{2,1,0:T(2,128)(2,1)} %reshape.211), calls=%async_computation.2 | async-start | bytes 524288 | tf_op jit(solution)/shard_map/all_to_all | solution.py:110
  39.8 0.8 copy.81
  42.0 7.0 %all-to-all-done.2 = bf16[4,2,16384]{2,1,0:T(2,128)(2,1)S(1)} async-done(((bf16[4,2,16384]{2,1,0:T(2,128)(2,1)}), bf16[4,2,16384]{2,1,0:T(2,128)(2,1)S(1)}, u32[]{:S(2)}, u32[]{:S(2)}) %all-to-all-start.2) | async-done | bytes 262176 | tf_op jit(solution)/shard_map/all_to_all | solution.py:110
  49.6 3.5 %fusion.114 = (f32[4,512]{1,0:T(4,128)S(1)}, f32[4,512,512]{1,2,0:T(8,128)}) fusion(bf16[512,4,64]{0,2,1:T(8,128)(2,1)S(1)} %reshape_squeeze.15, bf16[512,4,64]{0,2,1:T(8,128)(2,1)S(1)} %reshape_squeeze.16), kind=kOutput, calls=%fused_computation.236 | convolution fusion | flops 137363968 | bytes 4726784 | tf_op jit(solution)/shard_map/while/body/eval_jaxpr/sub | solution.py:20
  53.1 2.8 %fusion.6 = bf16[4,512,512]{1,2,0:T(8,128)(2,1)S(1)} fusion(f32[4,512,512]{1,2,0:T(8,128)} %get-tuple-element.138, f32[4,512]{1,0:T(4,128)S(1)} %get-tuple-element.137), kind=kLoop, calls=%fused_computation.38 | loop fusion | flops 2097152 | bytes 6299648 | tf_op jit(solution)/shard_map/while/body/eval_jaxpr/convert_element_type | solution.py:35
  56.8 2.3 reduce.7
  59.1 0.8 reshape.217
  59.8 3.6 %all-to-all-start.3 = ((bf16[4,2,16384]{2,1,0:T(2,128)(2,1)}), bf16[4,2,16384]{2,1,0:T(2,128)(2,1)S(1)}, u32[]{:S(2)}, u32[]{:S(2)}) async-start(bf16[4,2,16384]{2,1,0:T(2,128)(2,1)} %reshape.217), calls=%async_computation.3 | async-start | bytes 524288 | tf_op jit(solution)/shard_map/all_to_all | solution.py:113
  64.2 5.1 %all-to-all-done.3 = bf16[4,2,16384]{2,1,0:T(2,128)(2,1)S(1)} async-done(((bf16[4,2,16384]{2,1,0:T(2,128)(2,1)}), bf16[4,2,16384]{2,1,0:T(2,128)(2,1)S(1)}, u32[]{:S(2)}, u32[]{:S(2)}) %all-to-all-start.3) | async-done | bytes 262176 | tf_op jit(solution)/shard_map/all_to_all | solution.py:113
  69.7 1.1 fusion.105
  70.8 2.9 %fusion.4 = bf16[1,128,2048]{2,1,0:T(8,128)(2,1)S(1)} fusion(bf16[128,1024]{0,1:T(8,128)(2,1)S(1)} %fusion.105, bf16[1024,2048]{1,0:T(8,128)(2,1)} %all-gather.2.cloned.1.call-done), kind=kOutput, calls=%fused_computation.35 | convolution fusion | flops 537133056 | bytes 4980736 | tf_op jit(solution)/shard_map/dot_general | solution.py:123
  74.5 2.2 collective-permute-start
  77.3 0.8 copy.80
  78.2 1.8 copy.95
  80.0 0.9 pad_maximum_fusion.2
  81.0 3.2 %fusion.111 = (f32[128]{0:T(128)S(1)}, f32[1,128,1024]{2,1,0:T(8,128)S(1)}) fusion(f32[1,158,1024]{2,1,0:T(8,128)S(1)} %convert_element_type.110, f32[1024]{0:T(1024)} %bitcast.253, f32[1024]{0:T(1024)} %bitcast.255, f32[1024]{0:T(1024)S(1)} %bitcast.197, f32[1024]{0:T(1024)S(1)} %bitcast.199, f32[1024]{0:T(1024)S(1)} %bitcast.201, f32[1024]{0:T(1024)} %bitcast.203, ...), kind=kLoop, calls=%fused_computation.233 | loop fusion | flops 8126336 | bytes 16904704 | tf_op jit(solution)/shard_map/reduce_sum | solution.py:138
  84.5 1.8 multiply_reduce_fusion.1
  86.2 1.3 multiply_reduce_fusion.2
  87.5 0.8 multiply_reduce_fusion.20
  89.0 2.6 stack.127
  91.6 1.3 collective-permute-start.1
  92.9 43.4 %all-reduce = (f32[1024]{0:T(1024)}, f32[1024]{0:T(1024)}) all-reduce(f32[1024]{0:T(1024)} %get-tuple-element.93, f32[1024]{0:T(1024)} %get-tuple-element.96), channel_id=1, replica_groups=mesh['dp'=8,'seq'=4] {'dp','seq'}, use_global_device_ids=true, to_apply=%region_40.41 | all-reduce | flops 2048 | bytes 16384 | tf_op jit(solution)/shard_map/psum | solution.py:161
  136.3 1.3 broadcast_multiply_fusion.1
  137.6 3.6 %multiply_convert_fusion.1 = (bf16[1,128,1024]{2,1,0:T(8,128)(2,1)S(1)}, f32[1,128,1024]{2,1,0:T(8,128)S(1)}) fusion(bf16[1,128,2048]{2,1,0:T(8,128)(2,1)S(1)} %fusion.4, f32[1,128,1024]{2,1,0:T(8,128)S(1)} %get-tuple-element.99, f32[1024]{0:T(1024)} %bitcast.254, f32[1,30,1024]{2,1,0:T(8,128)S(1)} %collective-permute-done.1, f32[1024]{0:T(1024)} %bitcast.256, ...), kind=kLoop, calls=%fused_computation.210 | loop fusion | flops 12713984 | bytes 1822720 | tf_op jit(solution)/shard_map/convert.7
  141.9 3.7 %fusion.8 = bf16[1,128,1024]{2,1,0:T(8,128)(2,1)S(1)} fusion(bf16[1024,2048]{1,0:T(8,128)(2,1)} %all-gather.2.cloned.1.call-done, bf16[128,1024]{1,0:T(8,128)(2,1)S(1)} %bitcast.164, bf16[128,1024]{1,0:T(8,128)(2,1)S(1)} %bitcast.163, bf16[1,128,1024]{2,1,0:T(8,128)(2,1)} %param.15), kind=kOutput, calls=%fused_computation.74 | convolution fusion | flops 538312704 | bytes 5242880 | tf_op jit(solution)/shard_map/fc,dc->fd/dot_general | solution.py:178
  146.1 3.0 %reduce.8 = bf16[1024,128]{1,0:T(8,128)(2,1)} reduce(bf16[1024,1,128]{2,1,0:T(2,128)(2,1)S(1)} %bitcast.180, bf16[]{:T(256)} %broadcast.119), dimensions={1}, to_apply=%bitcast.135.reduce_sub_computation | reduce | bytes 524290
  149.0 1.7 reshape.219
  150.7 4.3 %all-to-all-start.4 = ((bf16[4,2,16384]{2,1,0:T(2,128)(2,1)}), bf16[4,2,16384]{2,1,0:T(2,128)(2,1)}, u32[]{:S(2)}, u32[]{:S(2)}) async-start(bf16[4,2,16384]{2,1,0:T(2,128)(2,1)} %reshape.219), calls=%async_computation.4 | async-start | bytes 524288 | tf_op jit(solution)/shard_map/all_to_all | solution.py:185
  155.0 61.4 %all-reduce.3.cloned.1.call-done = f32[31,1024]{1,0:T(8,128)} async-done(((f32[31,1024]{1,0:T(8,128)}), f32[31,1024]{1,0:T(8,128)}) %all-reduce.3.cloned.1.call-update) | async-done | bytes 126992 | tf_op jit(solution)/shard_map/psum | solution.py:161
  216.4 1.6 broadcast_multiply_fusion
  218.0 1.2 reshape.220
  219.5 1.5 convolution_convert_fusion.3
  221.1 3.1 %multiply_convert_fusion = bf16[4,512,512]{1,2,0:T(8,128)(2,1)S(1)} fusion(bf16[512,4,64]{0,2,1:T(8,128)(2,1)S(1)} %reshape_squeeze.18, bf16[512,4,64]{0,2,1:T(8,128)(2,1)S(1)} %copy-done.7, f32[4,512]{1,0:T(4,128)S(1)} %bitcast.288, f32[4,512,512]{1,2,0:T(8,128)} %get-tuple-element.138, f32[4,512]{1,0:T(4,128)S(1)} %copy-done.14), kind=kOutput, calls=%fused_computation.30 | convolution fusion | flops 139460608 | bytes 6832128 | tf_op jit(solution)/shard_map/while/body/eval_jaxpr/qhd,khd->hqk/dot_general | solution.py:69
  224.7 2.3 reduce.11
  226.9 0.8 reshape.225
  227.7 4.0 %all-to-all-start.7 = ((bf16[4,2,16384]{2,1,0:T(2,128)(2,1)}), bf16[4,2,16384]{2,1,0:T(2,128)(2,1)}, u32[]{:S(2)}, u32[]{:S(2)}) async-start(bf16[4,2,16384]{2,1,0:T(2,128)(2,1)} %reshape.225), calls=%async_computation.7 | async-start | bytes 524288 | tf_op jit(solution)/shard_map/all_to_all | solution.py:192
  231.7 1.7 convolution_convert_fusion.4
  233.9 2.3 reduce.10
  236.1 0.8 reshape.223
  236.9 0.9 all-to-all-done.7
  237.8 3.4 %all-to-all-start.6 = ((bf16[4,2,16384]{2,1,0:T(2,128)(2,1)}), bf16[4,2,16384]{2,1,0:T(2,128)(2,1)S(1)}, u32[]{:S(2)}, u32[]{:S(2)}) async-start(bf16[4,2,16384]{2,1,0:T(2,128)(2,1)} %reshape.223), calls=%async_computation.6 | async-start | bytes 524288 | tf_op jit(solution)/shard_map/all_to_all | solution.py:191
  241.2 1.4 convolution_convert_fusion.1
  243.1 2.3 reduce.9
  245.4 0.8 reshape.221
  246.1 1.1 all-to-all-done.6
  247.3 3.4 %all-to-all-start.5 = ((bf16[4,2,16384]{2,1,0:T(2,128)(2,1)}), bf16[4,2,16384]{2,1,0:T(2,128)(2,1)S(1)}, u32[]{:S(2)}, u32[]{:S(2)}) async-start(bf16[4,2,16384]{2,1,0:T(2,128)(2,1)} %reshape.221), calls=%async_computation.5 | async-start | bytes 524288 | tf_op jit(solution)/shard_map/all_to_all | solution.py:190
  250.7 0.8 pad_maximum_fusion.1
  251.5 1.2 reshape.226
  252.9 0.9 copy.98
  254.3 0.9 copy.97
  255.1 1.6 all-to-all-done.5
  257.2 0.9 copy.96
  (86 shorter events, 12.1 us)
Async XLA Ops:
  7.2 20.1 %copy-start.8 = (bf16[1,128,1024]{2,1,0:T(8,128)(2,1)S(1)}, bf16[1,128,1024]{2,1,0:T(8,128)(2,1)}, u32[]{:S(2)}) copy-start(bf16[1,128,1024]{2,1,0:T(8,128)(2,1)} %param.12) | copy-start | bytes 786436
  7.2 63.6 %all-gather.2.cloned.1.call-start = ((), (), s32[]{:S(2)}) async-start(), calls=%async_computation.8 | async-start | bytes 5242880 | tf_op jit(solution)/shard_map/all_gather | solution.py:125
  7.9 31.9 %copy-start.10 = (bf16[1,128,1024]{2,1,0:T(8,128)(2,1)S(1)}, bf16[1,128,1024]{2,1,0:T(8,128)(2,1)}, u32[]{:S(2)}) copy-start(bf16[1,128,1024]{2,1,0:T(8,128)(2,1)} %param.13) | copy-start | bytes 786436
  12.9 11.0 %all-to-all-start = ((bf16[4,2,16384]{2,1,0:T(2,128)(2,1)}), bf16[4,2,16384]{2,1,0:T(2,128)(2,1)S(1)}, u32[]{:S(2)}, u32[]{:S(2)}) async-start(bf16[4,2,16384]{2,1,0:T(2,128)(2,1)} %reshape.213), calls=%async_computation | async-start | bytes 524288 | tf_op jit(solution)/shard_map/all_to_all | solution.py:108
  23.9 12.5 %all-to-all-start.1 = ((bf16[4,2,16384]{2,1,0:T(2,128)(2,1)}), bf16[4,2,16384]{2,1,0:T(2,128)(2,1)S(1)}, u32[]{:S(2)}, u32[]{:S(2)}) async-start(bf16[4,2,16384]{2,1,0:T(2,128)(2,1)} %reshape.215), calls=%async_computation.1 | async-start | bytes 524288 | tf_op jit(solution)/shard_map/all_to_all | solution.py:109
  36.4 12.5 %all-to-all-start.2 = ((bf16[4,2,16384]{2,1,0:T(2,128)(2,1)}), bf16[4,2,16384]{2,1,0:T(2,128)(2,1)S(1)}, u32[]{:S(2)}, u32[]{:S(2)}) async-start(bf16[4,2,16384]{2,1,0:T(2,128)(2,1)} %reshape.211), calls=%async_computation.2 | async-start | bytes 524288 | tf_op jit(solution)/shard_map/all_to_all | solution.py:110
  41.3 11.8 %copy-start.5 = (bf16[512,4,64]{0,2,1:T(8,128)(2,1)}, bf16[512,4,64]{0,2,1:T(8,128)(2,1)S(1)}, u32[]{:S(2)}) copy-start(bf16[512,4,64]{0,2,1:T(8,128)(2,1)S(1)} %reshape_squeeze.15) | copy-start | bytes 786436
  42.0 11.1 %copy-start.4 = (bf16[512,4,64]{0,2,1:T(8,128)(2,1)}, bf16[512,4,64]{0,2,1:T(8,128)(2,1)S(1)}, u32[]{:S(2)}) copy-start(bf16[512,4,64]{0,2,1:T(8,128)(2,1)S(1)} %reshape_squeeze.16) | copy-start | bytes 786436
  49.6 6.3 %copy-start.6 = (bf16[512,4,64]{0,2,1:T(8,128)(2,1)}, bf16[512,4,64]{0,2,1:T(8,128)(2,1)S(1)}, u32[]{:S(2)}) copy-start(bf16[512,4,64]{0,2,1:T(8,128)(2,1)S(1)} %reshape_squeeze.17) | copy-start | bytes 786436
  53.1 3.3 %copy-start.13 = (f32[4,512]{1,0:T(4,128)}, f32[4,512]{1,0:T(4,128)S(1)}, u32[]{:S(2)}) copy-start(f32[4,512]{1,0:T(4,128)S(1)} %get-tuple-element.137) | copy-start | bytes 24580
  55.9 7.6 %copy-start.11 = (f32[31,1024]{1,0:T(8,128)S(1)}, f32[31,1024]{1,0:T(8,128)}, u32[]{:S(2)}) copy-start(f32[31,1024]{1,0:T(8,128)} %param.16) | copy-start | bytes 380932
  59.8 9.4 %all-to-all-start.3 = ((bf16[4,2,16384]{2,1,0:T(2,128)(2,1)}), bf16[4,2,16384]{2,1,0:T(2,128)(2,1)S(1)}, u32[]{:S(2)}, u32[]{:S(2)}) async-start(bf16[4,2,16384]{2,1,0:T(2,128)(2,1)} %reshape.217), calls=%async_computation.3 | async-start | bytes 524288 | tf_op jit(solution)/shard_map/all_to_all | solution.py:113
  63.4 153.0 %all-reduce.3.cloned.1.call-start = ((), (), s32[]{:S(2)}) async-start(), calls=%async_computation.9 | async-start | bytes 262144 | tf_op jit(solution)/shard_map/psum | solution.py:161
  74.5 5.4 %collective-permute-start = (bf16[1,30,1024]{2,1,0:T(8,128)(2,1)}, bf16[1,30,1024]{2,1,0:T(8,128)(2,1)}, u32[]{:S(2)}, u32[]{:S(2)}) collective-permute-start(bf16[1,30,1024]{2,1,0:T(8,128)(2,1)} %slice.448), channel_id=1, source_target_pairs={{0,1},{1,2},{2,3},{4,5},{5,6},{6,7},{8,9},{9,10},{10,11},{12,13},{... | collective-permute-start | bytes 184328 | tf_op jit(solution)/shard_map/ppermute | solution.py:12
  80.9 3.5 %copy-start.9 = (bf16[1,128,1024]{2,1,0:T(8,128)(2,1)S(1)}, bf16[1,128,1024]{2,1,0:T(8,128)(2,1)}, u32[]{:S(2)}) copy-start(bf16[1,128,1024]{2,1,0:T(8,128)(2,1)} %param.19) | copy-start | bytes 786436
  81.0 3.5 %copy-start.12 = (f32[1024]{0:T(1024)S(1)}, f32[1024]{0:T(1024)}, u32[]{:S(2)}) copy-start(f32[1024]{0:T(1024)} %param.17) | copy-start | bytes 12292
  81.0 3.5 %copy-start.15 = (f32[1024]{0:T(1024)S(1)}, f32[1024]{0:T(1024)}, u32[]{:S(2)}) copy-start(f32[1024]{0:T(1024)} %param.18) | copy-start | bytes 12292
  91.6 46.0 %collective-permute-start.1 = (f32[1,30,1024]{2,1,0:T(8,128)}, f32[1,30,1024]{2,1,0:T(8,128)S(1)}, u32[]{:S(2)}, u32[]{:S(2)}) collective-permute-start(f32[1,30,1024]{2,1,0:T(8,128)} %slice.480), channel_id=1, source_target_pairs={{1,0},{2,1},{3,2},{5,4},{6,5},{7,6},{9,8},{10,9},{11,10},{13,12},{... | collective-permute-start | bytes 368648 | tf_op jit(solution)/shard_map/ppermute | solution.py:12
  141.2 0.7 copy-start
  145.6 73.6 %copy-start.2 = (bf16[1,128,1024]{2,1,0:T(8,128)(2,1)}, bf16[1,128,1024]{2,1,0:T(8,128)(2,1)S(1)}, u32[]{:S(2)}) copy-start(bf16[1,128,1024]{2,1,0:T(8,128)(2,1)S(1)} %fusion.8) | copy-start | bytes 786436
  145.7 75.4 %copy-start.14 = (f32[4,512]{1,0:T(4,128)S(1)}, f32[4,512]{1,0:T(4,128)}, u32[]{:S(2)}) copy-start(f32[4,512]{1,0:T(4,128)} %copy-done.13) | copy-start | bytes 24580
  150.7 67.2 %all-to-all-start.4 = ((bf16[4,2,16384]{2,1,0:T(2,128)(2,1)}), bf16[4,2,16384]{2,1,0:T(2,128)(2,1)}, u32[]{:S(2)}, u32[]{:S(2)}) async-start(bf16[4,2,16384]{2,1,0:T(2,128)(2,1)} %reshape.219), calls=%async_computation.4 | async-start | bytes 524288 | tf_op jit(solution)/shard_map/all_to_all | solution.py:185
  219.2 1.9 copy-start.7
  221.1 3.1 %copy-start.3 = (bf16[4,64,512]{2,1,0:T(8,128)(2,1)S(1)}, bf16[4,64,512]{2,1,0:T(8,128)(2,1)}, u32[]{:S(2)}) copy-start(bf16[4,64,512]{2,1,0:T(8,128)(2,1)} %convolution_convert_fusion.3) | copy-start | bytes 786436
  227.7 10.1 %all-to-all-start.7 = ((bf16[4,2,16384]{2,1,0:T(2,128)(2,1)}), bf16[4,2,16384]{2,1,0:T(2,128)(2,1)}, u32[]{:S(2)}, u32[]{:S(2)}) async-start(bf16[4,2,16384]{2,1,0:T(2,128)(2,1)} %reshape.225), calls=%async_computation.7 | async-start | bytes 524288 | tf_op jit(solution)/shard_map/all_to_all | solution.py:192
  233.4 17.2 %copy-start.1 = (bf16[1,128,1024]{2,1,0:T(8,128)(2,1)S(1)}, bf16[1,128,1024]{2,1,0:T(8,128)(2,1)}, u32[]{:S(2)}) copy-start(bf16[1,128,1024]{2,1,0:T(8,128)(2,1)} %copy-done) | copy-start | bytes 786436
  237.8 9.4 %all-to-all-start.6 = ((bf16[4,2,16384]{2,1,0:T(2,128)(2,1)}), bf16[4,2,16384]{2,1,0:T(2,128)(2,1)S(1)}, u32[]{:S(2)}, u32[]{:S(2)}) async-start(bf16[4,2,16384]{2,1,0:T(2,128)(2,1)} %reshape.223), calls=%async_computation.6 | async-start | bytes 524288 | tf_op jit(solution)/shard_map/all_to_all | solution.py:191
  247.3 9.4 %all-to-all-start.5 = ((bf16[4,2,16384]{2,1,0:T(2,128)(2,1)}), bf16[4,2,16384]{2,1,0:T(2,128)(2,1)S(1)}, u32[]{:S(2)}, u32[]{:S(2)}) async-start(bf16[4,2,16384]{2,1,0:T(2,128)(2,1)} %reshape.221), calls=%async_computation.5 | async-start | bytes 524288 | tf_op jit(solution)/shard_map/all_to_all | solution.py:190
Sparse Core Ops, SparseCore 0:
  9.6 43.2 all-gather.1
  91.7 124.6 all-reduce.2
where the time goes:
time: 266 us; the launch traced here: 265 us
  waiting for transfers between devices  85.9 us (32%)
  blocking collectives  43.4 us (16%)
  other arithmetic  38.5 us (14%)
  starting transfers between devices  33.3 us (13%)
  local copies, waits for them, and re-layouts  30.8 us (12%)
  matrix products  18.3 us (7%)
  between operations  14.8 us (6%)
    psum x1, waiting for transfers between devices, shards(): lax.psum((kernel_term, gain_term, bias_term), ('dp', 'seq'))  61.4 us
    psum x1, blocking collectives, shards(): lax.psum((kernel_term, gain_term, bias_term), ('dp', 'seq'))  43.4 us
    unnamed x65, local copies, waits for them, and re-layouts  20.7 us
    unnamed x8, other arithmetic  18.7 us
    all_to_all x1, waiting for transfers between devices, shards(): lax.all_to_all(value_vecs, 'seq', split_axis=2, concat_axis=1, tiled=True)  6.95 us
    all_to_all x1, waiting for transfers between devices, shards(): lax.all_to_all(key_vecs, 'seq', split_axis=2, concat_axis=1, tiled=True)  5.69 us
  transfers between devices with their start and end apart: 12, of which 8 were waited for; matrix products, arithmetic and copies ran while one was open for 23% of the time, Pallas kernels for 0%

commit v1 on v0

--- a/solution.py
+++ b/solution.py
@@ -107,7 +107,12 @@
     query_heads, key_heads, value_heads = (
         lax.all_to_all(queries, "seq", split_axis=2, concat_axis=1, tiled=True),
         lax.all_to_all(key_vecs, "seq", split_axis=2, concat_axis=1, tiled=True),
-        lax.all_to_all(value_vecs, "seq", split_axis=2, concat_axis=1, tiled=True),
+        jnp.concatenate(
+            lax.all_to_all(
+                jnp.stack(jnp.split(value_vecs, lax.axis_size("seq"), axis=2)), "seq", 0, 0
+            ),
+            axis=1,
+        ),
     )
     context_local = attend_forward(query_heads[0], key_heads[0], value_heads[0], head_count)
     context_out = lax.all_to_all(

time: 266 us -> 261 us (0.981)
    all_to_all x1, waiting for transfers between devices: 6.95 us -> 1.15 us  [shards(): lax.all_to_all(jnp.stack(jnp.split(value_vecs, lax.axis_size('seq'), axis...]
    all_to_all x1, waiting for transfers between devices: 2.44 us -> 5.69 us  [shards(): lax.all_to_all(queries, 'seq', split_axis=2, concat_axis=1, tiled=True)]
    unnamed x65 -> x61, local copies, waits for them, and re-layouts: 20.7 us -> 18.3 us
    unnamed x8 -> x7, other arithmetic: 18.7 us -> 16.5 us
  transfers between devices with their start and end apart: 12 -> 12, of which waited for: 8 -> 8; matrix products, arithmetic and copies ran while one was open for 23% -> 22% of each run, Pallas kernels for 0% -> 0%
where the time goes in v1:
time: 261 us; the launch traced here: 260 us
  waiting for transfers between devices  84.9 us (33%)
  blocking collectives  42.6 us (16%)
  other arithmetic  37 us (14%)
  starting transfers between devices  33.1 us (13%)
  local copies, waits for them, and re-layouts  29.3 us (11%)
  matrix products  18.3 us (7%)
  between operations  14.8 us (6%)
    psum x1, waiting for transfers between devices, shards(): lax.psum((kernel_term, gain_term, bias_term), ('dp', 'seq'))  61.2 us
    psum x1, blocking collectives, shards(): lax.psum((kernel_term, gain_term, bias_term), ('dp', 'seq'))  42.6 us
    unnamed x61, local copies, waits for them, and re-layouts  18.3 us
    unnamed x7, other arithmetic  16.5 us
    all_to_all x1, waiting for transfers between devices, shards(): lax.all_to_all(key_vecs, 'seq', split_axis=2, concat_axis=1, tiled=True)  7.3 us
    all_to_all x1, waiting for transfers between devices, shards(): lax.all_to_all(queries, 'seq', split_axis=2, concat_axis=1, tiled=True)  5.69 us
    all_to_all x1, waiting for transfers between devices, shards(): lax.all_to_all(context_local[None], 'seq', split_axis=1, concat_axis=2, t...  5.26 us
  transfers between devices with their start and end apart: 12, of which 8 were waited for; matrix products, arithmetic and copies ran while one was open for 22% of the time, Pallas kernels for 0%

profile of v1, /device:TPU:0, one launch (start us, length us, event | category | flops | bytes accessed | tf_op | source)
XLA Modules:
  0.0 259.9 jit_solution(3094683049089259087)
XLA Ops:
  7.2 0.7 all-gather.2.cloned.1.call-update
  7.9 1.0 slice_bitcast_fusion.3
  8.9 0.7 pad_maximum_fusion.3
  9.6 4.2 %all-to-all-start = ((bf16[4,1,128,256]{3,2,1,0:T(8,128)(2,1)}), bf16[4,1,128,256]{3,2,1,0:T(8,128)(2,1)S(1)}, u32[]{:S(2)}, u32[]{:S(2)}) async-start(bf16[4,1,128,256]{3,2,1,0:T(8,128)(2,1)} %pad_maximum_fusion.3), calls=%async_computation | async-start | bytes 524288 | tf_op jit(solution)/shard_map/all_to_all | solution.py:111
  13.9 1.3 copy.71
  15.7 2.3 reduce.4
  18.0 0.8 reshape.210
  18.8 1.1 all-to-all-done
  19.9 3.4 %all-to-all-start.1 = ((bf16[4,2,16384]{2,1,0:T(2,128)(2,1)}), bf16[4,2,16384]{2,1,0:T(2,128)(2,1)S(1)}, u32[]{:S(2)}, u32[]{:S(2)}) async-start(bf16[4,2,16384]{2,1,0:T(2,128)(2,1)} %reshape.210), calls=%async_computation.1 | async-start | bytes 524288 | tf_op jit(solution)/shard_map/all_to_all | solution.py:108
  23.7 2.3 reduce.5
  26.0 0.8 reshape.212
  26.8 5.7 %all-to-all-done.1 = bf16[4,2,16384]{2,1,0:T(2,128)(2,1)S(1)} async-done(((bf16[4,2,16384]{2,1,0:T(2,128)(2,1)}), bf16[4,2,16384]{2,1,0:T(2,128)(2,1)S(1)}, u32[]{:S(2)}, u32[]{:S(2)}) %all-to-all-start.1) | async-done | bytes 262176 | tf_op jit(solution)/shard_map/all_to_all | solution.py:108
  32.5 3.4 %all-to-all-start.2 = ((bf16[4,2,16384]{2,1,0:T(2,128)(2,1)}), bf16[4,2,16384]{2,1,0:T(2,128)(2,1)S(1)}, u32[]{:S(2)}, u32[]{:S(2)}) async-start(bf16[4,2,16384]{2,1,0:T(2,128)(2,1)} %reshape.212), calls=%async_computation.2 | async-start | bytes 524288 | tf_op jit(solution)/shard_map/all_to_all | solution.py:109
  35.9 0.8 copy.78
  37.7 7.3 %all-to-all-done.2 = bf16[4,2,16384]{2,1,0:T(2,128)(2,1)S(1)} async-done(((bf16[4,2,16384]{2,1,0:T(2,128)(2,1)}), bf16[4,2,16384]{2,1,0:T(2,128)(2,1)S(1)}, u32[]{:S(2)}, u32[]{:S(2)}) %all-to-all-start.2) | async-done | bytes 262176 | tf_op jit(solution)/shard_map/all_to_all | solution.py:109
  45.7 3.5 %fusion.114 = (f32[4,512]{1,0:T(4,128)S(1)}, f32[4,512,512]{1,2,0:T(8,128)}) fusion(bf16[512,4,64]{0,2,1:T(8,128)(2,1)S(1)} %reshape_squeeze.11, bf16[512,4,64]{0,2,1:T(8,128)(2,1)S(1)} %reshape_squeeze.12), kind=kOutput, calls=%fused_computation.241 | convolution fusion | flops 137363968 | bytes 4726784 | tf_op jit(solution)/shard_map/while/body/eval_jaxpr/sub | solution.py:20
  49.2 2.8 %fusion.6 = bf16[4,512,512]{1,2,0:T(8,128)(2,1)S(1)} fusion(f32[4,512,512]{1,2,0:T(8,128)} %get-tuple-element.142, f32[4,512]{1,0:T(4,128)S(1)} %get-tuple-element.141), kind=kLoop, calls=%fused_computation.38 | loop fusion | flops 2097152 | bytes 6299648 | tf_op jit(solution)/shard_map/while/body/eval_jaxpr/convert_element_type | solution.py:35
  52.9 2.3 reduce.6
  55.1 0.8 reshape.214
  55.9 3.4 %all-to-all-start.3 = ((bf16[4,2,16384]{2,1,0:T(2,128)(2,1)}), bf16[4,2,16384]{2,1,0:T(2,128)(2,1)S(1)}, u32[]{:S(2)}, u32[]{:S(2)}) async-start(bf16[4,2,16384]{2,1,0:T(2,128)(2,1)} %reshape.214), calls=%async_computation.3 | async-start | bytes 524288 | tf_op jit(solution)/shard_map/all_to_all | solution.py:118
  60.1 5.3 %all-to-all-done.3 = bf16[4,2,16384]{2,1,0:T(2,128)(2,1)S(1)} async-done(((bf16[4,2,16384]{2,1,0:T(2,128)(2,1)}), bf16[4,2,16384]{2,1,0:T(2,128)(2,1)S(1)}, u32[]{:S(2)}, u32[]{:S(2)}) %all-to-all-start.3) | async-done | bytes 262176 | tf_op jit(solution)/shard_map/all_to_all | solution.py:118
  65.8 1.1 fusion.105
  66.9 2.9 %fusion.4 = bf16[1,128,2048]{2,1,0:T(8,128)(2,1)S(1)} fusion(bf16[128,1024]{0,1:T(8,128)(2,1)S(1)} %fusion.105, bf16[1024,2048]{1,0:T(8,128)(2,1)} %all-gather.2.cloned.1.call-done), kind=kOutput, calls=%fused_computation.35 | convolution fusion | flops 537133056 | bytes 4980736 | tf_op jit(solution)/shard_map/dot_general | solution.py:128
  70.6 2.1 collective-permute-start
  73.4 0.8 copy.77
  74.2 1.8 copy.92
  76.0 0.9 pad_maximum_fusion.2
  77.1 3.2 %fusion.111 = (f32[128]{0:T(128)S(1)}, f32[1,128,1024]{2,1,0:T(8,128)S(1)}) fusion(f32[1,158,1024]{2,1,0:T(8,128)S(1)} %convert_element_type.110, f32[1024]{0:T(1024)} %bitcast.253, f32[1024]{0:T(1024)} %bitcast.255, f32[1024]{0:T(1024)S(1)} %bitcast.197, f32[1024]{0:T(1024)S(1)} %bitcast.199, f32[1024]{0:T(1024)S(1)} %bitcast.201, f32[1024]{0:T(1024)} %bitcast.203, ...), kind=kLoop, calls=%fused_computation.238 | loop fusion | flops 8126336 | bytes 16904704 | tf_op jit(solution)/shard_map/reduce_sum | solution.py:143
  80.5 1.8 multiply_reduce_fusion.1
  82.3 1.3 multiply_reduce_fusion.2
  83.6 0.8 multiply_reduce_fusion.20
  85.0 2.6 stack.147
  87.6 1.3 collective-permute-start.1
  88.9 42.6 %all-reduce = (f32[1024]{0:T(1024)}, f32[1024]{0:T(1024)}) all-reduce(f32[1024]{0:T(1024)} %get-tuple-element.93, f32[1024]{0:T(1024)} %get-tuple-element.96), channel_id=1, replica_groups=mesh['dp'=8,'seq'=4] {'dp','seq'}, use_global_device_ids=true, to_apply=%region_40.41 | all-reduce | flops 2048 | bytes 16384 | tf_op jit(solution)/shard_map/psum | solution.py:166
  131.5 1.3 broadcast_multiply_fusion.1
  132.8 3.6 %multiply_convert_fusion.1 = (bf16[1,128,1024]{2,1,0:T(8,128)(2,1)S(1)}, f32[1,128,1024]{2,1,0:T(8,128)S(1)}) fusion(bf16[1,128,2048]{2,1,0:T(8,128)(2,1)S(1)} %fusion.4, f32[1,128,1024]{2,1,0:T(8,128)S(1)} %get-tuple-element.99, f32[1024]{0:T(1024)} %bitcast.254, f32[1,30,1024]{2,1,0:T(8,128)S(1)} %collective-permute-done.1, f32[1024]{0:T(1024)} %bitcast.256, ...), kind=kLoop, calls=%fused_computation.210 | loop fusion | flops 12713984 | bytes 1822720 | tf_op jit(solution)/shard_map/convert.7
  137.1 3.7 %fusion.8 = bf16[1,128,1024]{2,1,0:T(8,128)(2,1)S(1)} fusion(bf16[1024,2048]{1,0:T(8,128)(2,1)} %all-gather.2.cloned.1.call-done, bf16[128,1024]{1,0:T(8,128)(2,1)S(1)} %bitcast.167, bf16[128,1024]{1,0:T(8,128)(2,1)S(1)} %bitcast.166, bf16[1,128,1024]{2,1,0:T(8,128)(2,1)} %param.15), kind=kOutput, calls=%fused_computation.74 | convolution fusion | flops 538312704 | bytes 5242880 | tf_op jit(solution)/shard_map/fc,dc->fd/dot_general | solution.py:183
  141.3 3.0 %reduce.7 = bf16[1024,128]{1,0:T(8,128)(2,1)} reduce(bf16[1024,1,128]{2,1,0:T(2,128)(2,1)S(1)} %bitcast.181, bf16[]{:T(256)} %broadcast.119), dimensions={1}, to_apply=%bitcast.138.reduce_sub_computation | reduce | bytes 524290
  144.2 1.7 reshape.216
  146.0 4.3 %all-to-all-start.4 = ((bf16[4,2,16384]{2,1,0:T(2,128)(2,1)}), bf16[4,2,16384]{2,1,0:T(2,128)(2,1)}, u32[]{:S(2)}, u32[]{:S(2)}) async-start(bf16[4,2,16384]{2,1,0:T(2,128)(2,1)} %reshape.216), calls=%async_computation.4 | async-start | bytes 524288 | tf_op jit(solution)/shard_map/all_to_all | solution.py:190
  150.2 61.2 %all-reduce.3.cloned.1.call-done = f32[31,1024]{1,0:T(8,128)} async-done(((f32[31,1024]{1,0:T(8,128)}), f32[31,1024]{1,0:T(8,128)}) %all-reduce.3.cloned.1.call-update) | async-done | bytes 126992 | tf_op jit(solution)/shard_map/psum | solution.py:166
  211.4 1.6 broadcast_multiply_fusion
  213.0 1.2 reshape.217
  214.6 1.5 convolution_convert_fusion.2
  216.2 3.1 %multiply_convert_fusion = bf16[4,512,512]{1,2,0:T(8,128)(2,1)S(1)} fusion(bf16[512,4,64]{0,2,1:T(8,128)(2,1)S(1)} %reshape_squeeze.13, bf16[512,4,64]{0,2,1:T(8,128)(2,1)S(1)} %copy-done.7, f32[4,512]{1,0:T(4,128)S(1)} %bitcast.288, f32[4,512,512]{1,2,0:T(8,128)} %get-tuple-element.142, f32[4,512]{1,0:T(4,128)S(1)} %copy-done.14), kind=kOutput, calls=%fused_computation.30 | convolution fusion | flops 139460608 | bytes 6832128 | tf_op jit(solution)/shard_map/while/body/eval_jaxpr/qhd,khd->hqk/dot_general | solution.py:69
  219.7 2.3 reduce.10
  222.0 0.8 reshape.222
  222.7 4.0 %all-to-all-start.7 = ((bf16[4,2,16384]{2,1,0:T(2,128)(2,1)}), bf16[4,2,16384]{2,1,0:T(2,128)(2,1)}, u32[]{:S(2)}, u32[]{:S(2)}) async-start(bf16[4,2,16384]{2,1,0:T(2,128)(2,1)} %reshape.222), calls=%async_computation.7 | async-start | bytes 524288 | tf_op jit(solution)/shard_map/all_to_all | solution.py:197
  226.8 1.7 convolution_convert_fusion.3
  228.9 2.3 reduce.9
  231.2 0.8 reshape.220
  232.0 0.9 all-to-all-done.7
  232.9 3.4 %all-to-all-start.6 = ((bf16[4,2,16384]{2,1,0:T(2,128)(2,1)}), bf16[4,2,16384]{2,1,0:T(2,128)(2,1)S(1)}, u32[]{:S(2)}, u32[]{:S(2)}) async-start(bf16[4,2,16384]{2,1,0:T(2,128)(2,1)} %reshape.220), calls=%async_computation.6 | async-start | bytes 524288 | tf_op jit(solution)/shard_map/all_to_all | solution.py:196
  236.3 1.4 convolution_convert_fusion.1
  238.1 2.3 reduce.8
  240.4 0.8 reshape.218
  241.2 1.1 all-to-all-done.6
  242.3 3.4 %all-to-all-start.5 = ((bf16[4,2,16384]{2,1,0:T(2,128)(2,1)}), bf16[4,2,16384]{2,1,0:T(2,128)(2,1)S(1)}, u32[]{:S(2)}, u32[]{:S(2)}) async-start(bf16[4,2,16384]{2,1,0:T(2,128)(2,1)} %reshape.218), calls=%async_computation.5 | async-start | bytes 524288 | tf_op jit(solution)/shard_map/all_to_all | solution.py:195
  245.7 0.8 pad_maximum_fusion.1
  246.5 1.2 reshape.223
  248.0 0.9 copy.95
  249.3 0.9 copy.94
  250.2 1.5 all-to-all-done.5
  252.2 0.9 copy.93
  (83 shorter events, 11.1 us)
Async XLA Ops:
  7.2 16.2 %copy-start.8 = (bf16[1,128,1024]{2,1,0:T(8,128)(2,1)S(1)}, bf16[1,128,1024]{2,1,0:T(8,128)(2,1)}, u32[]{:S(2)}) copy-start(bf16[1,128,1024]{2,1,0:T(8,128)(2,1)} %param.11) | copy-start | bytes 786436
  7.2 28.7 %copy-start.10 = (bf16[1,128,1024]{2,1,0:T(8,128)(2,1)S(1)}, bf16[1,128,1024]{2,1,0:T(8,128)(2,1)}, u32[]{:S(2)}) copy-start(bf16[1,128,1024]{2,1,0:T(8,128)(2,1)} %param.13) | copy-start | bytes 786436
  7.2 59.7 %all-gather.2.cloned.1.call-start = ((), (), s32[]{:S(2)}) async-start(), calls=%async_computation.8 | async-start | bytes 5242880 | tf_op jit(solution)/shard_map/all_gather | solution.py:130
  9.6 10.3 %all-to-all-start = ((bf16[4,1,128,256]{3,2,1,0:T(8,128)(2,1)}), bf16[4,1,128,256]{3,2,1,0:T(8,128)(2,1)S(1)}, u32[]{:S(2)}, u32[]{:S(2)}) async-start(bf16[4,1,128,256]{3,2,1,0:T(8,128)(2,1)} %pad_maximum_fusion.3), calls=%async_computation | async-start | bytes 524288 | tf_op jit(solution)/shard_map/all_to_all | solution.py:111
  19.9 12.6 %all-to-all-start.1 = ((bf16[4,2,16384]{2,1,0:T(2,128)(2,1)}), bf16[4,2,16384]{2,1,0:T(2,128)(2,1)S(1)}, u32[]{:S(2)}, u32[]{:S(2)}) async-start(bf16[4,2,16384]{2,1,0:T(2,128)(2,1)} %reshape.210), calls=%async_computation.1 | async-start | bytes 524288 | tf_op jit(solution)/shard_map/all_to_all | solution.py:108
  32.5 12.5 %all-to-all-start.2 = ((bf16[4,2,16384]{2,1,0:T(2,128)(2,1)}), bf16[4,2,16384]{2,1,0:T(2,128)(2,1)S(1)}, u32[]{:S(2)}, u32[]{:S(2)}) async-start(bf16[4,2,16384]{2,1,0:T(2,128)(2,1)} %reshape.212), calls=%async_computation.2 | async-start | bytes 524288 | tf_op jit(solution)/shard_map/all_to_all | solution.py:109
  37.0 14.9 %copy-start.6 = (bf16[512,4,64]{0,2,1:T(8,128)(2,1)}, bf16[512,4,64]{0,2,1:T(8,128)(2,1)S(1)}, u32[]{:S(2)}) copy-start(bf16[512,4,64]{0,2,1:T(8,128)(2,1)S(1)} %reshape_squeeze_reshape.4) | copy-start | bytes 786436
  37.7 11.5 %copy-start.5 = (bf16[512,4,64]{0,2,1:T(8,128)(2,1)}, bf16[512,4,64]{0,2,1:T(8,128)(2,1)S(1)}, u32[]{:S(2)}) copy-start(bf16[512,4,64]{0,2,1:T(8,128)(2,1)S(1)} %reshape_squeeze.11) | copy-start | bytes 786436
  45.7 3.5 %copy-start.4 = (bf16[512,4,64]{0,2,1:T(8,128)(2,1)}, bf16[512,4,64]{0,2,1:T(8,128)(2,1)S(1)}, u32[]{:S(2)}) copy-start(bf16[512,4,64]{0,2,1:T(8,128)(2,1)S(1)} %reshape_squeeze.12) | copy-start | bytes 786436
  49.1 3.3 %copy-start.13 = (f32[4,512]{1,0:T(4,128)}, f32[4,512]{1,0:T(4,128)S(1)}, u32[]{:S(2)}) copy-start(f32[4,512]{1,0:T(4,128)S(1)} %get-tuple-element.141) | copy-start | bytes 24580
  51.9 7.4 %copy-start.11 = (f32[31,1024]{1,0:T(8,128)S(1)}, f32[31,1024]{1,0:T(8,128)}, u32[]{:S(2)}) copy-start(f32[31,1024]{1,0:T(8,128)} %param.16) | copy-start | bytes 380932
  55.9 9.4 %all-to-all-start.3 = ((bf16[4,2,16384]{2,1,0:T(2,128)(2,1)}), bf16[4,2,16384]{2,1,0:T(2,128)(2,1)S(1)}, u32[]{:S(2)}, u32[]{:S(2)}) async-start(bf16[4,2,16384]{2,1,0:T(2,128)(2,1)} %reshape.214), calls=%async_computation.3 | async-start | bytes 524288 | tf_op jit(solution)/shard_map/all_to_all | solution.py:118
  59.3 152.1 %all-reduce.3.cloned.1.call-start = ((), (), s32[]{:S(2)}) async-start(), calls=%async_computation.9 | async-start | bytes 262144 | tf_op jit(solution)/shard_map/psum | solution.py:166
  70.6 5.4 %collective-permute-start = (bf16[1,30,1024]{2,1,0:T(8,128)(2,1)}, bf16[1,30,1024]{2,1,0:T(8,128)(2,1)}, u32[]{:S(2)}, u32[]{:S(2)}) collective-permute-start(bf16[1,30,1024]{2,1,0:T(8,128)(2,1)} %slice.448), channel_id=1, source_target_pairs={{0,1},{1,2},{2,3},{4,5},{5,6},{6,7},{8,9},{9,10},{10,11},{12,13},{... | collective-permute-start | bytes 184328 | tf_op jit(solution)/shard_map/ppermute | solution.py:12
  77.0 3.5 %copy-start.9 = (bf16[1,128,1024]{2,1,0:T(8,128)(2,1)S(1)}, bf16[1,128,1024]{2,1,0:T(8,128)(2,1)}, u32[]{:S(2)}) copy-start(bf16[1,128,1024]{2,1,0:T(8,128)(2,1)} %param.19) | copy-start | bytes 786436
  77.0 3.5 %copy-start.12 = (f32[1024]{0:T(1024)S(1)}, f32[1024]{0:T(1024)}, u32[]{:S(2)}) copy-start(f32[1024]{0:T(1024)} %param.17) | copy-start | bytes 12292
  77.0 3.5 %copy-start.15 = (f32[1024]{0:T(1024)S(1)}, f32[1024]{0:T(1024)}, u32[]{:S(2)}) copy-start(f32[1024]{0:T(1024)} %param.18) | copy-start | bytes 12292
  87.6 45.2 %collective-permute-start.1 = (f32[1,30,1024]{2,1,0:T(8,128)}, f32[1,30,1024]{2,1,0:T(8,128)S(1)}, u32[]{:S(2)}, u32[]{:S(2)}) collective-permute-start(f32[1,30,1024]{2,1,0:T(8,128)} %slice.480), channel_id=1, source_target_pairs={{1,0},{2,1},{3,2},{5,4},{6,5},{7,6},{9,8},{10,9},{11,10},{13,12},{... | collective-permute-start | bytes 368648 | tf_op jit(solution)/shard_map/ppermute | solution.py:12
  136.4 0.7 copy-start
  140.9 73.4 %copy-start.2 = (bf16[1,128,1024]{2,1,0:T(8,128)(2,1)}, bf16[1,128,1024]{2,1,0:T(8,128)(2,1)S(1)}, u32[]{:S(2)}) copy-start(bf16[1,128,1024]{2,1,0:T(8,128)(2,1)S(1)} %fusion.8) | copy-start | bytes 786436
  140.9 75.3 %copy-start.14 = (f32[4,512]{1,0:T(4,128)S(1)}, f32[4,512]{1,0:T(4,128)}, u32[]{:S(2)}) copy-start(f32[4,512]{1,0:T(4,128)} %copy-done.13) | copy-start | bytes 24580
  146.0 67.1 %all-to-all-start.4 = ((bf16[4,2,16384]{2,1,0:T(2,128)(2,1)}), bf16[4,2,16384]{2,1,0:T(2,128)(2,1)}, u32[]{:S(2)}, u32[]{:S(2)}) async-start(bf16[4,2,16384]{2,1,0:T(2,128)(2,1)} %reshape.216), calls=%async_computation.4 | async-start | bytes 524288 | tf_op jit(solution)/shard_map/all_to_all | solution.py:190
  214.2 1.9 copy-start.7
  216.1 3.1 %copy-start.3 = (bf16[4,64,512]{2,1,0:T(8,128)(2,1)S(1)}, bf16[4,64,512]{2,1,0:T(8,128)(2,1)}, u32[]{:S(2)}) copy-start(bf16[4,64,512]{2,1,0:T(8,128)(2,1)} %convolution_convert_fusion.2) | copy-start | bytes 786436
  222.7 10.1 %all-to-all-start.7 = ((bf16[4,2,16384]{2,1,0:T(2,128)(2,1)}), bf16[4,2,16384]{2,1,0:T(2,128)(2,1)}, u32[]{:S(2)}, u32[]{:S(2)}) async-start(bf16[4,2,16384]{2,1,0:T(2,128)(2,1)} %reshape.222), calls=%async_computation.7 | async-start | bytes 524288 | tf_op jit(solution)/shard_map/all_to_all | solution.py:197
  228.5 17.2 %copy-start.1 = (bf16[1,128,1024]{2,1,0:T(8,128)(2,1)S(1)}, bf16[1,128,1024]{2,1,0:T(8,128)(2,1)}, u32[]{:S(2)}) copy-start(bf16[1,128,1024]{2,1,0:T(8,128)(2,1)} %copy-done) | copy-start | bytes 786436
  232.9 9.4 %all-to-all-start.6 = ((bf16[4,2,16384]{2,1,0:T(2,128)(2,1)}), bf16[4,2,16384]{2,1,0:T(2,128)(2,1)S(1)}, u32[]{:S(2)}, u32[]{:S(2)}) async-start(bf16[4,2,16384]{2,1,0:T(2,128)(2,1)} %reshape.220), calls=%async_computation.6 | async-start | bytes 524288 | tf_op jit(solution)/shard_map/all_to_all | solution.py:196
  242.3 9.4 %all-to-all-start.5 = ((bf16[4,2,16384]{2,1,0:T(2,128)(2,1)}), bf16[4,2,16384]{2,1,0:T(2,128)(2,1)S(1)}, u32[]{:S(2)}, u32[]{:S(2)}) async-start(bf16[4,2,16384]{2,1,0:T(2,128)(2,1)} %reshape.218), calls=%async_computation.5 | async-start | bytes 524288 | tf_op jit(solution)/shard_map/all_to_all | solution.py:195
Sparse Core Ops, SparseCore 0:
  9.6 42.7 all-gather.1
  87.8 123.6 all-reduce.2
